TPU v7x, 256 devices: a whole 4x4x8 slice. The times are simulated.
256 devices in a mesh: seq: 4 (over x), blk: 64 (over z, y, core).
Axes of the slice: x: 4, y: 4, z: 8, core: 2. Of those that a mesh axis runs over, the one named last changes fastest.
Arguments:
- queries: bfloat16 [32768, 3072], P(('blk', 'seq')), may hold values from -140 to 140
- key_states: bfloat16 [32768, 3072], P(('blk', 'seq')), may hold values from -4.5 to 4.5
- value_states: bfloat16 [32768, 3072], P(('blk', 'seq')), may hold values from -6 to 6
- grad_out: bfloat16 [32768, 3072], P(('blk', 'seq')), may hold values from -6 to 6
- clip_table: int32 [21, 4], replicated, may hold values from 0 to 511, as said below
- windows: int32 [21, 3], replicated, may hold values from 0 to 1
Outputs:
- attended: bfloat16 [32768, 3072], P(('blk', 'seq'))
- grad_queries: bfloat16 [32768, 3072], P(('blk', 'seq'))
- grad_keys: bfloat16 [32768, 3072], P(('blk', 'seq'))
- grad_values: bfloat16 [32768, 3072], P(('blk', 'seq'))
Inputs may be any that keep to these rules, and one draw needn't show every extreme that they name: `clip_table`: clips lie end to end from tile 0 and cover all 512 tiles; a clip's tiles run frame by frame, each frame row by row; heights and widths of tiles are 1 or 2.
All inputs are finite; a program needn't handle non-finite values.
Results may differ from a plain program's by a relative error of at most 0.012.
Values may be sent and summed in bfloat16 or wider, within the bound.
A program may use at most 128 MiB of HBM per device.

v0:
```python
import functools
import math

import jax
import jax.numpy as jnp
from jax import lax
from jax.experimental import pallas as pl
from jax.experimental.pallas import tpu as pltpu
from jax.sharding import PartitionSpec as P

HD = 128
TILE = 64
HALO = 448
MASKED = -1e30
MESH = pl.DeviceIdType.MESH


def nt(left, right):
    return lax.dot_general(
        left, right, (((1,), (1,)), ((), ())), preferred_element_type=jnp.float32
    )


def nn(left, right):
    return jnp.dot(left, right, preferred_element_type=jnp.float32)


def tn(left, right):
    return lax.dot_general(
        left, right, (((0,), (0,)), ((), ())), preferred_element_type=jnp.float32
    )


def fill_bias(bias, clip_table, windows, first_tile, total_tiles):
    shape = bias.shape
    q_tile = first_tile + lax.broadcasted_iota(jnp.int32, shape, 0)
    k_tile = first_tile - HALO // TILE + (lax.broadcasted_iota(jnp.int32, shape, 1) >> 6)
    none = jnp.full(shape, -1, jnp.int32)
    zero = jnp.zeros(shape, jnp.int32)
    one = jnp.ones(shape, jnp.int32)
    q_clip, k_clip, start = none, none, zero
    rows, cols = one, one
    reach_f, reach_r, reach_c = zero, zero, zero
    for clip in range(clip_table.shape[0]):
        begin = clip_table[clip, 0]
        here = q_tile >= begin
        q_clip = jnp.where(here, clip, q_clip)
        k_clip = jnp.where(k_tile >= begin, clip, k_clip)
        start = jnp.where(here, begin, start)
        rows = jnp.where(here, clip_table[clip, 2], rows)
        cols = jnp.where(here, clip_table[clip, 3], cols)
        reach_f = jnp.where(here, windows[clip, 0], reach_f)
        reach_r = jnp.where(here, windows[clip, 1], reach_r)
        reach_c = jnp.where(here, windows[clip, 2], reach_c)

    def place(tile):
        local = tile - start
        line = jnp.where(cols == 2, local >> 1, local)
        frame = jnp.where(rows == 2, line >> 1, line)
        return frame, line - frame * rows, local - line * cols

    q_frame, q_row, q_col = place(q_tile)
    k_frame, k_row, k_col = place(k_tile)
    allowed = (
        (q_clip == k_clip)
        & (k_tile >= 0)
        & (k_tile < total_tiles)
        & (jnp.abs(q_frame - k_frame) <= reach_f)
        & (jnp.abs(q_row - k_row) <= reach_r)
        & (jnp.abs(q_col - k_col) <= reach_c)
    )
    bias[...] = jnp.where(allowed, 0.0, MASKED).astype(jnp.float32)


def kernel(
    seq_axis,
    blk_axis,
    n_seq,
    n_blk,
    heads,
    q_in,
    k_in,
    v_in,
    g_in,
    clip_table,
    windows,
    att_out,
    dq_out,
    dk_out,
    dv_out,
    kv,
    qg,
    relay_in,
    results,
    relay_out,
    acc,
    rim_send,
    rim_recv,
    bias,
    in_recv,
    in_send,
    hop_recv,
    pass_send,
    halo_recv,
    halo_send,
    rim_recv_sem,
    rim_send_sem,
    out_recv,
    out_send,
    back_recv,
    back_send,
):
    scale = 1.0 / math.sqrt(HD)
    tok = q_in.shape[0]
    block = tok * n_seq
    me = lax.axis_index(seq_axis)
    blk = lax.axis_index(blk_axis)
    right = lax.rem(me + 1, n_seq)
    left = lax.rem(me + n_seq - 1, n_seq)
    far = lax.rem(me + 2, n_seq)
    above = lax.rem(blk + 1, n_blk)
    below = lax.rem(blk + n_blk - 1, n_blk)
    to_right, to_left = {seq_axis: right}, {seq_axis: left}
    to_above, to_below = {blk_axis: above}, {blk_axis: below}

    sources = (k_in, v_in, q_in, g_in)
    outs = (att_out, dq_out, dk_out, dv_out)

    def landing(array, stage, origin):
        row = origin * tok
        if array < 2:
            return kv.at[array, stage, pl.ds(HALO + row, tok), :]
        return qg.at[array - 2, stage, pl.ds(row, tok), :]

    def columns(ref, owner, stage):
        start = pl.multiple_of((owner * heads + stage) * HD, HD)
        return ref.at[:, pl.ds(start, HD)]

    def send(src, dst, send_sem, recv_sem, device):
        pltpu.make_async_remote_copy(
            src_ref=src,
            dst_ref=dst,
            send_sem=send_sem,
            recv_sem=recv_sem,
            device_id=device,
            device_id_type=MESH,
        ).start()

    def wait(ref, sem):
        pltpu.make_async_copy(ref, ref, sem).wait()

    def issue_in(stage):
        for array, src in enumerate(sources):
            via = to_right if array % 2 == 0 else to_left
            arrived = in_recv.at[stage, array]
            sent = in_send.at[array]
            send(
                columns(src, far, stage),
                relay_in.at[array, stage],
                sent,
                hop_recv.at[stage, array],
                via,
            )
            send(columns(src, right, stage), landing(array, stage, me), sent, arrived, to_right)
            send(columns(src, left, stage), landing(array, stage, me), sent, arrived, to_left)
            pltpu.make_async_copy(
                columns(src, me, stage), landing(array, stage, me), arrived
            ).start()

    def pass_in(stage):
        for array in range(4):
            wait(relay_in.at[array, stage], hop_recv.at[stage, array])
            onward, origin = (to_right, left) if array % 2 == 0 else (to_left, right)
            send(
                relay_in.at[array, stage],
                landing(array, stage, origin),
                pass_send.at[array],
                in_recv.at[stage, array],
                onward,
            )

    def send_halo(stage):
        for array in range(2):
            wait(kv.at[array, stage, pl.ds(HALO, block), :], in_recv.at[stage, array])
            sent = halo_send.at[array]
            send(
                kv.at[array, stage, pl.ds(block, HALO), :],
                kv.at[array, stage, pl.ds(0, HALO), :],
                sent,
                halo_recv.at[stage, array, 0],
                to_above,
            )
            send(
                kv.at[array, stage, pl.ds(HALO, HALO), :],
                kv.at[array, stage, pl.ds(HALO + block, HALO), :],
                sent,
                halo_recv.at[stage, array, 1],
                to_below,
            )

    def compute(stage):
        for array in range(2):
            wait(qg.at[array, stage], in_recv.at[stage, 2 + array])
            wait(kv.at[array, stage, pl.ds(0, HALO), :], halo_recv.at[stage, array, 0])
            wait(kv.at[array, stage, pl.ds(HALO + block, HALO), :], halo_recv.at[stage, array, 1])
        rows = block // 2
        span = rows + 2 * HALO
        for part in range(2):
            low = part * rows
            q = qg[0, stage, low : low + rows, :]
            g = qg[1, stage, low : low + rows, :]
            k = kv[0, stage, low : low + span, :]
            v = kv[1, stage, low : low + span, :]
            product = nt(q, k)
            per_part = rows // TILE
            scores = jnp.concatenate(
                [
                    product[t * TILE : (t + 1) * TILE] * scale
                    + bias[part * per_part + t : part * per_part + t + 1, low : low + span]
                    for t in range(per_part)
                ],
                axis=0,
            )
            row_max = jnp.max(scores, axis=1, keepdims=True)
            weights = jnp.exp(scores - row_max)
            total = jnp.sum(weights, axis=1, keepdims=True)
            probs = weights * (1.0 / total)
            probs_low = probs.astype(jnp.bfloat16)
            attended = nn(probs_low, v).astype(jnp.bfloat16)
            delta = jnp.sum(
                g.astype(jnp.float32) * attended.astype(jnp.float32), axis=1, keepdims=True
            )
            dscores = (probs * (nt(g, v) - delta) * scale).astype(jnp.bfloat16)
            results[0, stage, low : low + rows, :] = attended
            results[1, stage, low : low + rows, :] = nn(dscores, k).astype(jnp.bfloat16)
            for index, grad in enumerate((tn(dscores, q), tn(probs_low, g))):
                if part == 0:
                    acc[index, stage, 0:span, :] = grad
                else:
                    shared = span - rows
                    acc[index, stage, rows:span, :] += grad[:shared]
                    acc[index, stage, span : span + rows, :] = grad[shared:]
        for index in range(2):
            rim_send[index, stage, 0] = acc[index, stage, 0:HALO, :].astype(jnp.bfloat16)
            rim_send[index, stage, 1] = acc[
                index, stage, HALO + block : 2 * HALO + block, :
            ].astype(jnp.bfloat16)
            sent = rim_send_sem.at[index]
            send(
                rim_send.at[index, stage, 0],
                rim_recv.at[index, stage, 1],
                sent,
                rim_recv_sem.at[stage, index, 1],
                to_below,
            )
            send(
                rim_send.at[index, stage, 1],
                rim_recv.at[index, stage, 0],
                sent,
                rim_recv_sem.at[stage, index, 0],
                to_above,
            )

    def finish(stage):
        for index in range(2):
            wait(rim_recv.at[index, stage, 0], rim_recv_sem.at[stage, index, 0])
            wait(rim_recv.at[index, stage, 1], rim_recv_sem.at[stage, index, 1])
            edge = block - HALO
            acc[index, stage, HALO : 2 * HALO, :] += rim_recv[index, stage, 0].astype(jnp.float32)
            acc[index, stage, HALO + edge : HALO + block, :] += rim_recv[index, stage, 1].astype(
                jnp.float32
            )
            results[2 + index, stage] = acc[index, stage, HALO : HALO + block, :].astype(
                jnp.bfloat16
            )

    def rows_of(array, stage, owner):
        return results.at[array, stage, pl.ds(pl.multiple_of(owner * tok, tok), tok), :]

    def issue_out(stage, arrays):
        for array in arrays:
            via = to_right if array % 2 == 0 else to_left
            arrived = out_recv.at[array]
            sent = out_send.at[array]
            mine = columns(outs[array], me, stage)
            send(
                rows_of(array, stage, far),
                relay_out.at[array, stage],
                sent,
                back_recv.at[stage, array],
                via,
            )
            send(rows_of(array, stage, right), mine, sent, arrived, to_right)
            send(rows_of(array, stage, left), mine, sent, arrived, to_left)
            pltpu.make_async_copy(rows_of(array, stage, me), mine, arrived).start()

    def pass_out(stage, arrays):
        for array in arrays:
            wait(relay_out.at[array, stage], back_recv.at[stage, array])
            onward, origin = (to_right, left) if array % 2 == 0 else (to_left, right)
            send(
                relay_out.at[array, stage],
                columns(outs[array], origin, stage),
                back_send.at[array],
                out_recv.at[array],
                onward,
            )

    barrier = pltpu.get_barrier_semaphore()
    for device in (to_right, to_left, to_above, to_below):
        pl.semaphore_signal(barrier, inc=1, device_id=device, device_id_type=MESH)
    pl.semaphore_wait(barrier, 4)

    issue_in(0)
    issue_in(1)
    tiles = block // TILE
    fill_bias(bias, clip_table, windows, blk * tiles, n_blk * tiles)

    def step(index, carry):
        def run(lag, action):
            stage = index - lag

            @pl.when((stage >= 0) & (stage < heads))
            def _():
                action(stage)

        run(0, pass_in)
        run(-2, lambda stage: pl.when(stage >= 2)(lambda: issue_in(stage)))
        run(0, send_halo)
        run(1, compute)
        run(2, finish)
        run(2, lambda stage: issue_out(stage, range(4)))
        run(3, lambda stage: pass_out(stage, range(4)))
        return carry

    lax.fori_loop(0, heads + 3, step, 0)

    for array in range(4):
        wait(outs[array], out_recv.at[array])
        wait(sources[array].at[:, pl.ds(0, 3 * heads * HD)], in_send.at[array])
        wait(relay_in.at[array], pass_send.at[array])
        wait(results.at[array, :, pl.ds(0, 3 * tok), :], out_send.at[array])
        wait(relay_out.at[array], back_send.at[array])
    for index in range(2):
        wait(rim_send.at[index], halo_send.at[index])
        wait(rim_send.at[index], rim_send_sem.at[index])


def on_device(n_seq, n_blk, queries, key_states, value_states, grad_out, clip_table, windows):
    tok, width = queries.shape
    heads = width // HD // n_seq
    block = tok * n_seq
    extended = block + 2 * HALO
    low = jnp.bfloat16
    hbm = pl.BlockSpec(memory_space=pl.ANY)
    smem = pl.BlockSpec(memory_space=pltpu.SMEM)
    dma = pltpu.SemaphoreType.DMA
    return pl.pallas_call(
        functools.partial(kernel, "seq", "blk", n_seq, n_blk, heads),
        out_shape=[jax.ShapeDtypeStruct((tok, width), low)] * 4,
        in_specs=[hbm] * 4 + [smem] * 2,
        out_specs=[hbm] * 4,
        scratch_shapes=[
            pltpu.VMEM((2, heads, extended, HD), low),
            pltpu.VMEM((2, heads, block, HD), low),
            pltpu.VMEM((4, heads, tok, HD), low),
            pltpu.VMEM((4, heads, block, HD), low),
            pltpu.VMEM((4, heads, tok, HD), low),
            pltpu.VMEM((2, heads, extended, HD), jnp.float32),
            pltpu.VMEM((2, heads, 2, HALO, HD), low),
            pltpu.VMEM((2, heads, 2, HALO, HD), low),
            pltpu.VMEM((block // TILE, extended), jnp.float32),
            dma((heads, 4)),
            dma((4,)),
            dma((heads, 4)),
            dma((4,)),
            dma((heads, 2, 2)),
            dma((2,)),
            dma((heads, 2, 2)),
            dma((2,)),
            dma((4,)),
            dma((4,)),
            dma((heads, 4)),
            dma((4,)),
        ],
        compiler_params=pltpu.CompilerParams(
            collective_id=0, has_side_effects=True, vmem_limit_bytes=60 * 1024 * 1024
        ),
        name="attention_with_exchange",
    )(queries, key_states, value_states, grad_out, clip_table, windows)


def solution(mesh):
    rows = P(("blk", "seq"), None)
    return jax.shard_map(
        functools.partial(on_device, mesh.shape["seq"], mesh.shape["blk"]),
        mesh=mesh,
        in_specs=(rows, rows, rows, rows, P(), P()),
        out_specs=(rows, rows, rows, rows),
        check_vma=False,
    )
```

profile of v0, /device:TPU:4, one launch (start us, length us, event | category | flops | bytes accessed | tf_op | source)
XLA Modules:
  0.0 97.0 jit_solution(12771510370321350862)
XLA Ops:
  0.6 0.0 copy-start.3
  0.6 1.4 %copy.10.clip_table = s32[21,4]{1,0:T(8,128)} copy(s32[21,4]{0,1:T(4,128)} %param.10) | data formatting | bytes 672 | tf_op args[4]
  2.0 0.0 copy-done.3
  2.0 0.7 copy.11.windows
  2.7 88.5 %attention_with_exchange.1 = (bf16[128,3072]{1,0:T(8,128)(2,1)}, bf16[128,3072]{1,0:T(8,128)(2,1)}, bf16[128,3072]{1,0:T(8,128)(2,1)}, bf16[128,3072]{1,0:T(8,128)(2,1)}) custom-call(bf16[128,3072]{1,0:T(8,128)(2,1)} %q_in.1, bf16[128,3072]{1,0:T(8,128)(2,1)} %k_in.1, bf16[128,3072]{1,0:T(8,128)(2,1)} %v_in.1, bf16[128,3072]{1,0:T(8,128)(2,1)} %g_in.1, ...), custom_call_target="tpu_custom_call" | custom-call | tf_op jit(solution)/shard_map/attention_with_exchange/pallas_call | solution.py:358
  91.2 0.0 copy-start.2
  91.2 2.1 %copy.16 = bf16[128,3072]{1,0:T(8,128)(2,1)} copy(bf16[128,3072]{1,0:T(8,128)(2,1)} %get-tuple-element.8) | data formatting | bytes 1572864
  93.3 0.0 copy-done.2
  93.3 0.0 copy-start.1
  93.3 0.9 copy.17
  94.2 0.5 copy-done.1
  94.7 0.0 copy-start
  94.7 0.9 copy.18
  95.6 0.5 copy-done
  96.1 0.9 copy.19
Async XLA Ops:
  0.6 1.4 %copy-start.3 = (s32[21,3]{0,1:T(4,128)S(1)}, s32[21,3]{0,1:T(4,128)}, u32[]{:S(2)}) copy-start(s32[21,3]{0,1:T(4,128)} %param.11) | copy-start | bytes 760
  91.2 2.1 %copy-start.2 = (bf16[128,3072]{1,0:T(8,128)(2,1)S(1)}, bf16[128,3072]{1,0:T(8,128)(2,1)}, u32[]{:S(2)}) copy-start(bf16[128,3072]{1,0:T(8,128)(2,1)} %get-tuple-element.9) | copy-start | bytes 2359300
  93.3 1.4 %copy-start.1 = (bf16[128,3072]{1,0:T(8,128)(2,1)S(1)}, bf16[128,3072]{1,0:T(8,128)(2,1)}, u32[]{:S(2)}) copy-start(bf16[128,3072]{1,0:T(8,128)(2,1)} %get-tuple-element.10) | copy-start | bytes 2359300
  94.7 1.4 %copy-start = (bf16[128,3072]{1,0:T(8,128)(2,1)S(1)}, bf16[128,3072]{1,0:T(8,128)(2,1)}, u32[]{:S(2)}) copy-start(bf16[128,3072]{1,0:T(8,128)(2,1)} %get-tuple-element.11) | copy-start | bytes 2359300
where the time goes:
time: 97.3 us; the launch traced here: 97 us
  Pallas kernels  88.5 us (91%)
  local copies, waits for them, and re-layouts  7.91 us (8%)
    pallas_call x1, Pallas kernels, on_device(): pl.pallas_call(functools.partial(kernel, 'seq', 'blk', n_seq, n_blk, head...  88.5 us
    unnamed x14, local copies, waits for them, and re-layouts  7.91 us

commit v1 on v0

--- a/solution.py
+++ b/solution.py
@@ -152,15 +152,16 @@
     def issue_in(stage):
         for array, src in enumerate(sources):
             via = to_right if array % 2 == 0 else to_left
+            send(
+                columns(src, far, stage),
+                relay_in.at[array, stage],
+                in_send.at[array],
+                hop_recv.at[stage, array],
+                via,
+            )
+        for array, src in enumerate(sources):
             arrived = in_recv.at[stage, array]
             sent = in_send.at[array]
-            send(
-                columns(src, far, stage),
-                relay_in.at[array, stage],
-                sent,
-                hop_recv.at[stage, array],
-                via,
-            )
             send(columns(src, right, stage), landing(array, stage, me), sent, arrived, to_right)
             send(columns(src, left, stage), landing(array, stage, me), sent, arrived, to_left)
             pltpu.make_async_copy(
@@ -280,16 +281,17 @@
     def issue_out(stage, arrays):
         for array in arrays:
             via = to_right if array % 2 == 0 else to_left
+            send(
+                rows_of(array, stage, far),
+                relay_out.at[array, stage],
+                out_send.at[array],
+                back_recv.at[stage, array],
+                via,
+            )
+        for array in arrays:
             arrived = out_recv.at[array]
             sent = out_send.at[array]
             mine = columns(outs[array], me, stage)
-            send(
-                rows_of(array, stage, far),
-                relay_out.at[array, stage],
-                sent,
-                back_recv.at[stage, array],
-                via,
-            )
             send(rows_of(array, stage, right), mine, sent, arrived, to_right)
             send(rows_of(array, stage, left), mine, sent, arrived, to_left)
             pltpu.make_async_copy(rows_of(array, stage, me), mine, arrived).start()
@@ -312,28 +314,32 @@
     pl.semaphore_wait(barrier, 4)
 
     issue_in(0)
-    issue_in(1)
     tiles = block // TILE
     fill_bias(bias, clip_table, windows, blk * tiles, n_blk * tiles)
+    pass_in(0)
+    issue_in(1)
+    send_halo(0)
+    pass_in(1)
+    issue_in(2)
 
     def step(index, carry):
-        def run(lag, action):
-            stage = index - lag
+        def run(ahead, action):
+            stage = index + ahead
 
             @pl.when((stage >= 0) & (stage < heads))
             def _():
                 action(stage)
 
-        run(0, pass_in)
-        run(-2, lambda stage: pl.when(stage >= 2)(lambda: issue_in(stage)))
-        run(0, send_halo)
-        run(1, compute)
-        run(2, finish)
-        run(2, lambda stage: issue_out(stage, range(4)))
-        run(3, lambda stage: pass_out(stage, range(4)))
+        run(1, send_halo)
+        run(2, pass_in)
+        run(3, issue_in)
+        run(0, compute)
+        run(-1, finish)
+        run(-1, lambda stage: issue_out(stage, range(4)))
+        run(-2, lambda stage: pass_out(stage, range(4)))
         return carry
 
-    lax.fori_loop(0, heads + 3, step, 0)
+    lax.fori_loop(0, heads + 2, step, 0)
 
     for array in range(4):
         wait(outs[array], out_recv.at[array])

time: 97.3 us -> 85.6 us (0.88)
  Pallas kernels: 88.5 us -> 76.7 us
    pallas_call x1, Pallas kernels: 88.5 us -> 76.7 us  [on_device(): pl.pallas_call(functools.partial(kernel, 'seq', 'blk', n_seq, n_blk, head...]
where the time goes in v1:
time: 85.6 us; the launch traced here: 85.3 us
  Pallas kernels  76.7 us (90%)
  local copies, waits for them, and re-layouts  7.91 us (9%)
    pallas_call x1, Pallas kernels, on_device(): pl.pallas_call(functools.partial(kernel, 'seq', 'blk', n_seq, n_blk, head...  76.7 us
    unnamed x14, local copies, waits for them, and re-layouts  7.91 us

profile of v1, /device:TPU:4, one launch (start us, length us, event | category | flops | bytes accessed | tf_op | source)
XLA Modules:
  0.0 85.3 jit_solution(1702464316988735990)
XLA Ops:
  0.6 0.0 copy-start.3
  0.6 1.4 %copy.10.clip_table = s32[21,4]{1,0:T(8,128)} copy(s32[21,4]{0,1:T(4,128)} %param.10) | data formatting | bytes 672 | tf_op args[4]
  2.0 0.0 copy-done.3
  2.0 0.7 copy.11.windows
  2.7 76.7 %attention_with_exchange.1 = (bf16[128,3072]{1,0:T(8,128)(2,1)}, bf16[128,3072]{1,0:T(8,128)(2,1)}, bf16[128,3072]{1,0:T(8,128)(2,1)}, bf16[128,3072]{1,0:T(8,128)(2,1)}) custom-call(bf16[128,3072]{1,0:T(8,128)(2,1)} %q_in.1, bf16[128,3072]{1,0:T(8,128)(2,1)} %k_in.1, bf16[128,3072]{1,0:T(8,128)(2,1)} %v_in.1, bf16[128,3072]{1,0:T(8,128)(2,1)} %g_in.1, ...), custom_call_target="tpu_custom_call" | custom-call | tf_op jit(solution)/shard_map/attention_with_exchange/pallas_call | solution.py:364
  79.4 0.0 copy-start.2
  79.4 2.1 %copy.16 = bf16[128,3072]{1,0:T(8,128)(2,1)} copy(bf16[128,3072]{1,0:T(8,128)(2,1)} %get-tuple-element.8) | data formatting | bytes 1572864
  81.5 0.0 copy-done.2
  81.6 0.0 copy-start.1
  81.6 0.9 %copy.17 = bf16[128,3072]{1,0:T(8,128)(2,1)} copy(bf16[128,3072]{1,0:T(8,128)(2,1)S(1)} %copy-done.2) | data formatting | bytes 1572864
  82.4 0.5 copy-done.1
  83.0 0.0 copy-start
  83.0 0.9 %copy.18 = bf16[128,3072]{1,0:T(8,128)(2,1)} copy(bf16[128,3072]{1,0:T(8,128)(2,1)S(1)} %copy-done.1) | data formatting | bytes 1572864
  83.9 0.5 copy-done
  84.4 0.9 %copy.19 = bf16[128,3072]{1,0:T(8,128)(2,1)} copy(bf16[128,3072]{1,0:T(8,128)(2,1)S(1)} %copy-done) | data formatting | bytes 1572864
Async XLA Ops:
  0.6 1.4 %copy-start.3 = (s32[21,3]{0,1:T(4,128)S(1)}, s32[21,3]{0,1:T(4,128)}, u32[]{:S(2)}) copy-start(s32[21,3]{0,1:T(4,128)} %param.11) | copy-start | bytes 760
  79.4 2.1 %copy-start.2 = (bf16[128,3072]{1,0:T(8,128)(2,1)S(1)}, bf16[128,3072]{1,0:T(8,128)(2,1)}, u32[]{:S(2)}) copy-start(bf16[128,3072]{1,0:T(8,128)(2,1)} %get-tuple-element.9) | copy-start | bytes 2359300
  81.6 1.4 %copy-start.1 = (bf16[128,3072]{1,0:T(8,128)(2,1)S(1)}, bf16[128,3072]{1,0:T(8,128)(2,1)}, u32[]{:S(2)}) copy-start(bf16[128,3072]{1,0:T(8,128)(2,1)} %get-tuple-element.10) | copy-start | bytes 2359300
  83.0 1.4 %copy-start = (bf16[128,3072]{1,0:T(8,128)(2,1)S(1)}, bf16[128,3072]{1,0:T(8,128)(2,1)}, u32[]{:S(2)}) copy-start(bf16[128,3072]{1,0:T(8,128)(2,1)} %get-tuple-element.11) | copy-start | bytes 2359300

commit v2 on v1

--- a/solution.py
+++ b/solution.py
@@ -12,6 +12,7 @@
 TILE = 64
 HALO = 448
 MASKED = -1e30
+PIECE = 32
 MESH = pl.DeviceIdType.MESH
 
 
@@ -41,17 +42,17 @@
     q_clip, k_clip, start = none, none, zero
     rows, cols = one, one
     reach_f, reach_r, reach_c = zero, zero, zero
-    for clip in range(clip_table.shape[0]):
-        begin = clip_table[clip, 0]
+    for clip in range(clip_table.shape[1]):
+        begin = clip_table[0, clip]
         here = q_tile >= begin
         q_clip = jnp.where(here, clip, q_clip)
         k_clip = jnp.where(k_tile >= begin, clip, k_clip)
         start = jnp.where(here, begin, start)
-        rows = jnp.where(here, clip_table[clip, 2], rows)
-        cols = jnp.where(here, clip_table[clip, 3], cols)
-        reach_f = jnp.where(here, windows[clip, 0], reach_f)
-        reach_r = jnp.where(here, windows[clip, 1], reach_r)
-        reach_c = jnp.where(here, windows[clip, 2], reach_c)
+        rows = jnp.where(here, clip_table[2, clip], rows)
+        cols = jnp.where(here, clip_table[3, clip], cols)
+        reach_f = jnp.where(here, windows[0, clip], reach_f)
+        reach_r = jnp.where(here, windows[1, clip], reach_r)
+        reach_c = jnp.where(here, windows[2, clip], reach_c)
 
     def place(tile):
         local = tile - start
@@ -352,6 +353,32 @@
         wait(rim_send.at[index], rim_send_sem.at[index])
 
 
+def hand_over(*refs):
+    inner, outer, held, (arrived, left) = refs[:4], refs[4:8], refs[8], refs[9:]
+    tok = held.shape[1]
+    pieces = [(array, row) for row in range(0, tok, PIECE) for array in range(4)]
+
+    def take(array, row):
+        rows = pl.ds(row, PIECE)
+        return pltpu.make_async_copy(
+            inner[array].at[rows], held.at[array, rows], arrived.at[array, row // PIECE]
+        )
+
+    def put(array, row):
+        rows = pl.ds(row, PIECE)
+        return pltpu.make_async_copy(
+            held.at[array, rows], outer[array].at[rows], left.at[array, row // PIECE]
+        )
+
+    for piece in pieces:
+        take(*piece).start()
+    for piece in pieces:
+        take(*piece).wait()
+        put(*piece).start()
+    for piece in pieces:
+        put(*piece).wait()
+
+
 def on_device(n_seq, n_blk, queries, key_states, value_states, grad_out, clip_table, windows):
     tok, width = queries.shape
     heads = width // HD // n_seq
@@ -361,7 +388,7 @@
     hbm = pl.BlockSpec(memory_space=pl.ANY)
     smem = pl.BlockSpec(memory_space=pltpu.SMEM)
     dma = pltpu.SemaphoreType.DMA
-    return pl.pallas_call(
+    inner = pl.pallas_call(
         functools.partial(kernel, "seq", "blk", n_seq, n_blk, heads),
         out_shape=[jax.ShapeDtypeStruct((tok, width), low)] * 4,
         in_specs=[hbm] * 4 + [smem] * 2,
@@ -393,7 +420,19 @@
             collective_id=0, has_side_effects=True, vmem_limit_bytes=60 * 1024 * 1024
         ),
         name="attention_with_exchange",
-    )(queries, key_states, value_states, grad_out, clip_table, windows)
+    )(queries, key_states, value_states, grad_out, clip_table.T, windows.T)
+    return pl.pallas_call(
+        hand_over,
+        out_shape=[jax.ShapeDtypeStruct((tok, width), low)] * 4,
+        in_specs=[hbm] * 4,
+        out_specs=[hbm] * 4,
+        scratch_shapes=[
+            pltpu.VMEM((4, tok, width), low),
+            dma((4, tok // PIECE)),
+            dma((4, tok // PIECE)),
+        ],
+        name="hand_over",
+    )(*inner)
 
 
 def solution(mesh):

time: 85.6 us -> 80.4 us (0.939)
  local copies, waits for them, and re-layouts: 7.91 us -> 0 us
  Pallas kernels: 76.7 us -> 79.7 us
    unnamed x14 -> x0, local copies, waits for them, and re-layouts: 7.91 us -> none
    pallas_call x0 -> x1, Pallas kernels: none -> 3.18 us  [on_device(): pl.pallas_call(hand_over, out_shape=[jax.ShapeDtypeStruct((tok, width), l...]
where the time goes in v2:
time: 80.4 us; the launch traced here: 80.3 us
  Pallas kernels  79.7 us (99%)
    pallas_call x1, Pallas kernels, on_device(): pl.pallas_call(functools.partial(kernel, 'seq', 'blk', n_seq, n_blk, head...  76.5 us
    pallas_call x1, Pallas kernels, on_device(): pl.pallas_call(hand_over, out_shape=[jax.ShapeDtypeStruct((tok, width), l...  3.18 us

profile of v2, /device:TPU:4, one launch (start us, length us, event | category | flops | bytes accessed | tf_op | source)
XLA Modules:
  0.0 80.3 jit_solution(94606694226930248)
XLA Ops:
  0.6 76.5 %attention_with_exchange.1 = (bf16[128,3072]{1,0:T(8,128)(2,1)}, bf16[128,3072]{1,0:T(8,128)(2,1)}, bf16[128,3072]{1,0:T(8,128)(2,1)}, bf16[128,3072]{1,0:T(8,128)(2,1)}) custom-call(bf16[128,3072]{1,0:T(8,128)(2,1)} %q_in.1, bf16[128,3072]{1,0:T(8,128)(2,1)} %k_in.1, bf16[128,3072]{1,0:T(8,128)(2,1)} %v_in.1, bf16[128,3072]{1,0:T(8,128)(2,1)} %g_in.1, ...), custom_call_target="tpu_custom_call" | custom-call | tf_op jit(solution)/shard_map/attention_with_exchange/pallas_call | solution.py:391
  77.1 3.2 %hand_over.1 = (bf16[128,3072]{1,0:T(8,128)(2,1)}, bf16[128,3072]{1,0:T(8,128)(2,1)}, bf16[128,3072]{1,0:T(8,128)(2,1)}, bf16[128,3072]{1,0:T(8,128)(2,1)}) custom-call(bf16[128,3072]{1,0:T(8,128)(2,1)} %get-tuple-element.8.refs_0_, bf16[128,3072]{1,0:T(8,128)(2,1)} %get-tuple-element.9.refs_1_, bf16[128,3072]{1,0:T(8,128)(2,1)} %get-tuple-element.10.refs_2_, ...), custom_call_target="tpu_custom_call" | custom-call | tf_op jit(solution)/shard_map/hand_over/pallas_call | solution.py:424

commit v3 on v2

--- a/solution.py
+++ b/solution.py
@@ -200,7 +200,7 @@
                 to_below,
             )
 
-    def compute(stage):
+    def compute(stage, between):
         for array in range(2):
             wait(qg.at[array, stage], in_recv.at[stage, 2 + array])
             wait(kv.at[array, stage, pl.ds(0, HALO), :], halo_recv.at[stage, array, 0])
@@ -208,6 +208,8 @@
         rows = block // 2
         span = rows + 2 * HALO
         for part in range(2):
+            if part == 1:
+                between()
             low = part * rows
             q = qg[0, stage, low : low + rows, :]
             g = qg[1, stage, low : low + rows, :]
@@ -331,13 +333,17 @@
             def _():
                 action(stage)
 
-        run(1, send_halo)
-        run(2, pass_in)
-        run(3, issue_in)
-        run(0, compute)
+        def arrivals():
+            run(1, send_halo)
+            run(2, pass_in)
+            run(3, issue_in)
+
+        run(0, lambda stage: compute(stage, arrivals))
+        run(0, lambda stage: issue_out(stage, (0, 1)))
+        run(-2, lambda stage: pass_out(stage, (0, 1)))
         run(-1, finish)
-        run(-1, lambda stage: issue_out(stage, range(4)))
-        run(-2, lambda stage: pass_out(stage, range(4)))
+        run(-1, lambda stage: issue_out(stage, (2, 3)))
+        run(-2, lambda stage: pass_out(stage, (2, 3)))
         return carry
 
     lax.fori_loop(0, heads + 2, step, 0)

time: 80.4 us -> 83.7 us (1.041)
  Pallas kernels: 79.7 us -> 83 us
    pallas_call x1, Pallas kernels: 76.5 us -> 79.8 us  [on_device(): pl.pallas_call(functools.partial(kernel, 'seq', 'blk', n_seq, n_blk, head...]
where the time goes in v3:
time: 83.7 us; the launch traced here: 83.6 us
  Pallas kernels  83 us (99%)
    pallas_call x1, Pallas kernels, on_device(): pl.pallas_call(functools.partial(kernel, 'seq', 'blk', n_seq, n_blk, head...  79.8 us
    pallas_call x1, Pallas kernels, on_device(): pl.pallas_call(hand_over, out_shape=[jax.ShapeDtypeStruct((tok, width), l...  3.18 us

profile of v3, /device:TPU:4, one launch (start us, length us, event | category | flops | bytes accessed | tf_op | source)
XLA Modules:
  0.0 83.6 jit_solution(638564664619896171)
XLA Ops:
  0.6 79.8 %attention_with_exchange.1 = (bf16[128,3072]{1,0:T(8,128)(2,1)}, bf16[128,3072]{1,0:T(8,128)(2,1)}, bf16[128,3072]{1,0:T(8,128)(2,1)}, bf16[128,3072]{1,0:T(8,128)(2,1)}) custom-call(bf16[128,3072]{1,0:T(8,128)(2,1)} %q_in.1, bf16[128,3072]{1,0:T(8,128)(2,1)} %k_in.1, bf16[128,3072]{1,0:T(8,128)(2,1)} %v_in.1, bf16[128,3072]{1,0:T(8,128)(2,1)} %g_in.1, ...), custom_call_target="tpu_custom_call" | custom-call | tf_op jit(solution)/shard_map/attention_with_exchange/pallas_call | solution.py:397
  80.4 3.2 %hand_over.1 = (bf16[128,3072]{1,0:T(8,128)(2,1)}, bf16[128,3072]{1,0:T(8,128)(2,1)}, bf16[128,3072]{1,0:T(8,128)(2,1)}, bf16[128,3072]{1,0:T(8,128)(2,1)}) custom-call(bf16[128,3072]{1,0:T(8,128)(2,1)} %get-tuple-element.8.refs_0_, bf16[128,3072]{1,0:T(8,128)(2,1)} %get-tuple-element.9.refs_1_, bf16[128,3072]{1,0:T(8,128)(2,1)} %get-tuple-element.10.refs_2_, ...), custom_call_target="tpu_custom_call" | custom-call | tf_op jit(solution)/shard_map/hand_over/pallas_call | solution.py:430

commit v4 on v2

--- a/solution.py
+++ b/solution.py
@@ -217,14 +217,14 @@
             per_part = rows // TILE
             scores = jnp.concatenate(
                 [
-                    product[t * TILE : (t + 1) * TILE] * scale
+                    product[t * TILE : (t + 1) * TILE]
                     + bias[part * per_part + t : part * per_part + t + 1, low : low + span]
                     for t in range(per_part)
                 ],
                 axis=0,
             )
             row_max = jnp.max(scores, axis=1, keepdims=True)
-            weights = jnp.exp(scores - row_max)
+            weights = jnp.exp2((scores - row_max) * (scale * math.log2(math.e)))
             total = jnp.sum(weights, axis=1, keepdims=True)
             probs = weights * (1.0 / total)
             probs_low = probs.astype(jnp.bfloat16)
@@ -232,10 +232,10 @@
             delta = jnp.sum(
                 g.astype(jnp.float32) * attended.astype(jnp.float32), axis=1, keepdims=True
             )
-            dscores = (probs * (nt(g, v) - delta) * scale).astype(jnp.bfloat16)
+            dscores = (probs * (nt(g, v) - delta)).astype(jnp.bfloat16)
             results[0, stage, low : low + rows, :] = attended
-            results[1, stage, low : low + rows, :] = nn(dscores, k).astype(jnp.bfloat16)
-            for index, grad in enumerate((tn(dscores, q), tn(probs_low, g))):
+            results[1, stage, low : low + rows, :] = (nn(dscores, k) * scale).astype(jnp.bfloat16)
+            for index, grad in enumerate((tn(dscores, q) * scale, tn(probs_low, g))):
                 if part == 0:
                     acc[index, stage, 0:span, :] = grad
                 else:

time: 80.4 us -> 80.4 us (level)
  no operation moved by 1% of the time
where the time goes in v4:
time: 80.4 us; the launch traced here: 80.3 us
  Pallas kernels  79.6 us (99%)
    pallas_call x1, Pallas kernels, on_device(): pl.pallas_call(functools.partial(kernel, 'seq', 'blk', n_seq, n_blk, head...  76.5 us
    pallas_call x1, Pallas kernels, on_device(): pl.pallas_call(hand_over, out_shape=[jax.ShapeDtypeStruct((tok, width), l...  3.18 us

profile of v4, /device:TPU:4, one launch (start us, length us, event | category | flops | bytes accessed | tf_op | source)
XLA Modules:
  0.0 80.3 jit_solution(16884636531273095427)
XLA Ops:
  0.6 76.5 %attention_with_exchange.1 = (bf16[128,3072]{1,0:T(8,128)(2,1)}, bf16[128,3072]{1,0:T(8,128)(2,1)}, bf16[128,3072]{1,0:T(8,128)(2,1)}, bf16[128,3072]{1,0:T(8,128)(2,1)}) custom-call(bf16[128,3072]{1,0:T(8,128)(2,1)} %q_in.1, bf16[128,3072]{1,0:T(8,128)(2,1)} %k_in.1, bf16[128,3072]{1,0:T(8,128)(2,1)} %v_in.1, bf16[128,3072]{1,0:T(8,128)(2,1)} %g_in.1, ...), custom_call_target="tpu_custom_call" | custom-call | tf_op jit(solution)/shard_map/attention_with_exchange/pallas_call | solution.py:391
  77.1 3.2 %hand_over.1 = (bf16[128,3072]{1,0:T(8,128)(2,1)}, bf16[128,3072]{1,0:T(8,128)(2,1)}, bf16[128,3072]{1,0:T(8,128)(2,1)}, bf16[128,3072]{1,0:T(8,128)(2,1)}) custom-call(bf16[128,3072]{1,0:T(8,128)(2,1)} %get-tuple-element.8.refs_0_, bf16[128,3072]{1,0:T(8,128)(2,1)} %get-tuple-element.9.refs_1_, bf16[128,3072]{1,0:T(8,128)(2,1)} %get-tuple-element.10.refs_2_, ...), custom_call_target="tpu_custom_call" | custom-call | tf_op jit(solution)/shard_map/hand_over/pallas_call | solution.py:424
